TPU v7x, 128 devices: a whole 4x4x4 slice. The times are simulated.
128 devices in a mesh: seq: 32 (over z, x, core), head: 4 (over y).
Axes of the slice: x: 4, y: 4, z: 4, core: 2. Of those that a mesh axis runs over, the one named last changes fastest.
Arguments:
- inputs: bfloat16 [32768, 2048], P('seq', 'head'), may hold values from -6 to 6
- w_qkv: bfloat16 [3, 2048, 2048], P(None, None, 'head'), may hold values from -0.125 to 0.125
- level_weight: float32 [16, 6], P('head'), may hold values from 0.5 to 2
- grad_out: bfloat16 [32768, 2048], P('seq', 'head'), may hold values from -6 to 6
Outputs:
- attn_out: bfloat16 [32768, 2048], P('seq', 'head')
- grad_query: bfloat16 [32768, 2048], P('seq', 'head')
- grad_key: bfloat16 [32768, 2048], P('seq', 'head')
- grad_value: bfloat16 [32768, 2048], P('seq', 'head')
All inputs are finite; a program needn't handle non-finite values.
Results may differ from a plain program's by a relative error of at most 0.012.
Values may be sent and summed in bfloat16 or wider, within the bound.
A program may use at most 128 MiB of HBM per device.

v0:
```python
import math
import jax
import jax.numpy as jnp
from jax import lax
from jax.sharding import PartitionSpec as P


def partner(value, axis, stride):
    mask = 2**stride
    pairs = [(source, source ^ mask) for source in range(lax.axis_size(axis))]
    return lax.ppermute(value, axis, pairs)


def per_device(inputs, w_qkv, level_weight, grad_out):
    rows = inputs.shape[0]
    head_count = level_weight.shape[0]
    width = w_qkv.shape[2]
    head_size = width // head_count
    projected = jnp.einsum(
        "tn,jnf->jtf",
        lax.all_gather(inputs, "head", axis=1, tiled=True),
        w_qkv,
        preferred_element_type=jnp.float32,
    ).astype(jnp.bfloat16)
    queries = projected[0].reshape(rows, head_count, head_size)
    keys = projected[1].reshape(rows, head_count, head_size)
    values = projected[2].reshape(rows, head_count, head_size)
    grad_rows = grad_out.reshape(rows, head_count, head_size)
    key_state = jnp.einsum("thd,the->hde", keys, values, preferred_element_type=jnp.float32)
    query_state = jnp.einsum("thd,the->hde", queries, grad_rows, preferred_element_type=jnp.float32)
    position = lax.axis_index("seq")
    depth = lax.axis_size("seq").bit_length() - 1

    def level_coef(bit_level):
        return level_weight[:, bit_level + 1] / math.sqrt(head_size * rows * 2**bit_level)

    forward_mix = jnp.zeros((head_count, head_size, head_size), jnp.float32)
    backward_mix = jnp.zeros((head_count, head_size, head_size), jnp.float32)
    running = key_state
    for bit_level in range(depth):
        partner_sum = partner(running.astype(jnp.bfloat16), "seq", bit_level).astype(running.dtype)
        bit_on = position >> bit_level & 1 == 1
        forward_mix = forward_mix + jnp.where(
            bit_on, level_coef(bit_level)[:, None, None] * partner_sum, 0.0
        )
        running = running + partner_sum
    running = query_state
    for bit_level in range(depth):
        partner_sum = partner(running.astype(jnp.bfloat16), "seq", bit_level).astype(running.dtype)
        bit_on = position >> bit_level & 1 == 1
        backward_mix = backward_mix + jnp.where(
            bit_on, 0.0, level_coef(bit_level)[:, None, None] * partner_sum
        )
        running = running + partner_sum
    forward_low = forward_mix.astype(jnp.bfloat16)
    backward_low = backward_mix.astype(jnp.bfloat16)
    local_scale = (level_weight[:, 0] / math.sqrt(head_size * rows))[:, None, None]
    causal = (jnp.arange(rows)[:, None] >= jnp.arange(rows)[None, :])[None]
    scores = jnp.einsum("thd,shd->hts", queries, keys, preferred_element_type=jnp.float32)
    attend = jnp.where(causal, scores * local_scale, 0.0).astype(jnp.bfloat16)
    grad_scores = jnp.einsum("the,she->hts", grad_rows, values, preferred_element_type=jnp.float32)
    grad_attend = jnp.where(causal, grad_scores * local_scale, 0.0).astype(jnp.bfloat16)
    output = jnp.einsum("hts,she->the", attend, values, preferred_element_type=jnp.float32)
    output = output + jnp.einsum(
        "thd,hde->the", queries, forward_low, preferred_element_type=jnp.float32
    )
    grad_q = jnp.einsum("hts,shd->thd", grad_attend, keys, preferred_element_type=jnp.float32)
    grad_q = grad_q + jnp.einsum(
        "the,hde->thd", grad_rows, forward_low, preferred_element_type=jnp.float32
    )
    grad_k = jnp.einsum("hts,thd->shd", grad_attend, queries, preferred_element_type=jnp.float32)
    grad_k = grad_k + jnp.einsum(
        "the,hde->thd", values, backward_low, preferred_element_type=jnp.float32
    )
    grad_v = jnp.einsum("hts,the->she", attend, grad_rows, preferred_element_type=jnp.float32)
    grad_v = grad_v + jnp.einsum(
        "thd,hde->the", keys, backward_low, preferred_element_type=jnp.float32
    )
    return (
        output.reshape(rows, width).astype(jnp.bfloat16),
        grad_q.reshape(rows, width).astype(jnp.bfloat16),
        grad_k.reshape(rows, width).astype(jnp.bfloat16),
        grad_v.reshape(rows, width).astype(jnp.bfloat16),
    )


def solution(mesh):
    in_specs = (P("seq", "head"), P(None, None, "head"), P("head", None), P("seq", "head"))
    out_specs = (P("seq", "head"), P("seq", "head"), P("seq", "head"), P("seq", "head"))
    return jax.shard_map(
        per_device, mesh=mesh, in_specs=in_specs, out_specs=out_specs, check_vma=False
    )
```

profile of v0, /device:TPU:0, one launch (start us, length us, event | category | flops | bytes accessed | tf_op | source)
XLA Modules:
  0.0 144.0 jit_solution(12768049927329601054)
XLA Ops:
  9.4 1.6 %multiply_reduce_fusion.4 = (f32[4]{0:T(128)S(1)}, f32[4]{0:T(128)S(1)}, f32[4]{0:T(128)S(1)}, f32[4]{0:T(128)S(1)}, f32[4]{0:T(128)S(1)}, /*index=5*/f32[4]{0:T(128)}) fusion(f32[4,6]{1,0:T(4,128)} %param.6), kind=kLoop, calls=%fused_computation.56 | loop fusion | flops 24 | bytes 192 | tf_op jit(solution)/shard_map/div | solution.py:35
  12.3 48.1 %all-gather.2.cloned.1.call-done = bf16[1024,2048]{1,0:T(8,128)(2,1)} async-done(((bf16[1024,512]{1,0:T(8,128)(2,1)}), bf16[1024,2048]{1,0:T(8,128)(2,1)}) %all-gather.2.cloned.1.call-update) | async-done | bytes 4194320 | tf_op jit(solution)/shard_map/all_gather | solution.py:21
  60.4 10.3 %convert_bitcast_fusion = bf16[3,1024,512]{1,2,0:T(8,128)(2,1)S(1)} fusion(bf16[3,2048,512]{2,1,0:T(8,128)(2,1)} %param.5, bf16[1024,2048]{1,0:T(8,128)(2,1)} %all-gather.2.cloned.1.call-done), kind=kOutput, calls=%fused_computation.6 | convolution fusion | flops 6444023808 | bytes 13631488 | tf_op jit(solution)/shard_map/tn,jnf->jtf/dot_general | solution.py:19
  71.9 3.1 %fusion = bf16[4,1024,1024]{2,1,0:T(8,128)(2,1)S(1)} fusion(bf16[1024,4,128]{0,2,1:T(8,128)(2,1)S(1)} %bitcast.53, bf16[1024,4,128]{0,2,1:T(8,128)(2,1)S(1)} %bitcast.65, f32[4]{0:T(128)S(1)} %get-tuple-element.11, pred[1024,1024]{1,0:T(8,128)(4,1)S(1)} %copy-done.10), kind=kOutput, calls=%fused_computation.1 | convolution fusion | flops 1086324736 | bytes 11534352 | tf_op jit(solution)/shard_map/the,she->hts/dot_general | solution.py:61
  75.0 2.6 %fusion.42 = f32[4,128,1024]{2,1,0:T(8,128)} fusion(bf16[1024,4,128]{0,2,1:T(8,128)(2,1)S(1)} %bitcast.61, bf16[4,1024,1024]{2,1,0:T(8,128)(2,1)S(1)} %fusion), kind=kOutput, calls=%fused_computation.66 | convolution fusion | flops 1073741824 | bytes 11534336 | tf_op jit(solution)/shard_map/hts,thd->shd/dot_general | solution.py:71
  77.7 2.9 %fusion.41 = f32[4,128,1024]{2,1,0:T(8,128)S(1)} fusion(bf16[1024,4,128]{0,2,1:T(8,128)(2,1)S(1)} %bitcast.57, bf16[4,1024,1024]{2,1,0:T(8,128)(2,1)S(1)} %fusion), kind=kOutput, calls=%fused_computation.65 | convolution fusion | flops 1073741824 | bytes 11534336 | tf_op jit(solution)/shard_map/hts,shd->thd/dot_general | solution.py:67
  80.6 3.1 %select_convert_fusion = bf16[4,1024,1024]{2,1,0:T(8,128)(2,1)S(1)} fusion(bf16[1024,4,128]{0,2,1:T(8,128)(2,1)S(1)} %bitcast.62, bf16[1024,4,128]{0,2,1:T(8,128)(2,1)S(1)} %bitcast.58, f32[4]{0:T(128)S(1)} %get-tuple-element.11, pred[1024,1024]{1,0:T(8,128)(4,1)S(1)} %copy-done.10), kind=kOutput, calls=%fused_computation.2 | convolution fusion | flops 1086324736 | bytes 11534352 | tf_op jit(solution)/shard_map/thd,shd->hts/dot_general | solution.py:59
  84.3 4.3 %fusion.40 = f32[4,128,1024]{2,1,0:T(8,128)} fusion(bf16[1024,4,128]{0,2,1:T(8,128)(2,1)S(1)} %bitcast.66, bf16[4,1024,1024]{2,1,0:T(8,128)(2,1)S(1)} %select_convert_fusion), kind=kOutput, calls=%fused_computation.64 | convolution fusion | flops 1073741824 | bytes 11534336 | tf_op jit(solution)/shard_map/hts,she->the/dot_general | solution.py:63
  88.6 1.6 %collective-permute-start.1 = (bf16[4,128,128]{2,1,0:T(8,128)(2,1)S(1)}, bf16[4,128,128]{2,1,0:T(8,128)(2,1)S(1)}, u32[]{:S(2)}, u32[]{:S(2)}) collective-permute-start(bf16[4,128,128]{2,1,0:T(8,128)(2,1)S(1)} %fusion.26), channel_id=1, source_target_pairs={{0,8},{4,12},{8,0},{12,4},{16,24},{20,28},{24,16},{28,20},{32,40},... | collective-permute-start | bytes 393224 | tf_op jit(solution)/shard_map/ppermute | solution.py:11
  90.9 4.2 %collective-permute-done.1 = bf16[4,128,128]{2,1,0:T(8,128)(2,1)S(1)} collective-permute-done((bf16[4,128,128]{2,1,0:T(8,128)(2,1)S(1)}, bf16[4,128,128]{2,1,0:T(8,128)(2,1)S(1)}, u32[]{:S(2)}, u32[]{:S(2)}) %collective-permute-start.1) | collective-permute-done | bytes 131104 | tf_op jit(solution)/shard_map/ppermute | solution.py:11
  95.1 3.1 %collective-permute-start.2 = (bf16[4,128,128]{2,1,0:T(8,128)(2,1)S(1)}, bf16[4,128,128]{2,1,0:T(8,128)(2,1)S(1)}, u32[]{:S(2)}, u32[]{:S(2)}) collective-permute-start(bf16[4,128,128]{2,1,0:T(8,128)(2,1)S(1)} %fusion.30), channel_id=1, source_target_pairs={{0,16},{4,20},{8,24},{12,28},{16,0},{20,4},{24,8},{28,12},{32,48},... | collective-permute-start | bytes 393224 | tf_op jit(solution)/shard_map/ppermute | solution.py:11
  98.2 2.1 %collective-permute-start.7 = (bf16[4,128,128]{2,1,0:T(8,128)(2,1)S(1)}, bf16[4,128,128]{2,1,0:T(8,128)(2,1)S(1)}, u32[]{:S(2)}, u32[]{:S(2)}) collective-permute-start(bf16[4,128,128]{2,1,0:T(8,128)(2,1)S(1)} %fusion.31), channel_id=1, source_target_pairs={{0,16},{4,20},{8,24},{12,28},{16,0},{20,4},{24,8},{28,12},{32,48},... | collective-permute-start | bytes 393224 | tf_op jit(solution)/shard_map/ppermute | solution.py:11
  100.4 2.7 %collective-permute-done.2 = bf16[4,128,128]{2,1,0:T(8,128)(2,1)S(1)} collective-permute-done((bf16[4,128,128]{2,1,0:T(8,128)(2,1)S(1)}, bf16[4,128,128]{2,1,0:T(8,128)(2,1)S(1)}, u32[]{:S(2)}, u32[]{:S(2)}) %collective-permute-start.2) | collective-permute-done | bytes 131104 | tf_op jit(solution)/shard_map/ppermute | solution.py:11
  103.2 1.6 %collective-permute-start.3 = (bf16[4,128,128]{2,1,0:T(8,128)(2,1)S(1)}, bf16[4,128,128]{2,1,0:T(8,128)(2,1)S(1)}, u32[]{:S(2)}, u32[]{:S(2)}) collective-permute-start(bf16[4,128,128]{2,1,0:T(8,128)(2,1)S(1)} %fusion.27), channel_id=1, source_target_pairs={{0,32},{4,36},{8,40},{12,44},{16,48},{20,52},{24,56},{28,60},{32,0... | collective-permute-start | bytes 393224 | tf_op jit(solution)/shard_map/ppermute | solution.py:11
  105.0 1.6 %collective-permute-start.8 = (bf16[4,128,128]{2,1,0:T(8,128)(2,1)S(1)}, bf16[4,128,128]{2,1,0:T(8,128)(2,1)S(1)}, u32[]{:S(2)}, u32[]{:S(2)}) collective-permute-start(bf16[4,128,128]{2,1,0:T(8,128)(2,1)S(1)} %fusion.29), channel_id=1, source_target_pairs={{0,32},{4,36},{8,40},{12,44},{16,48},{20,52},{24,56},{28,60},{32,0... | collective-permute-start | bytes 393224 | tf_op jit(solution)/shard_map/ppermute | solution.py:11
  106.7 2.7 %collective-permute-done.3 = bf16[4,128,128]{2,1,0:T(8,128)(2,1)S(1)} collective-permute-done((bf16[4,128,128]{2,1,0:T(8,128)(2,1)S(1)}, bf16[4,128,128]{2,1,0:T(8,128)(2,1)S(1)}, u32[]{:S(2)}, u32[]{:S(2)}) %collective-permute-start.3) | collective-permute-done | bytes 131104 | tf_op jit(solution)/shard_map/ppermute | solution.py:11
  109.5 3.4 %collective-permute-start.4 = (bf16[4,128,128]{2,1,0:T(8,128)(2,1)S(1)}, bf16[4,128,128]{2,1,0:T(8,128)(2,1)S(1)}, u32[]{:S(2)}, u32[]{:S(2)}) collective-permute-start(bf16[4,128,128]{2,1,0:T(8,128)(2,1)S(1)} %fusion.15), channel_id=1, source_target_pairs={{0,64},{4,68},{8,72},{12,76},{16,80},{20,84},{24,88},{28,92},{32,9... | collective-permute-start | bytes 393224 | tf_op jit(solution)/shard_map/ppermute | solution.py:11
  113.7 2.4 %collective-permute-start.9 = (bf16[4,128,128]{2,1,0:T(8,128)(2,1)}, bf16[4,128,128]{2,1,0:T(8,128)(2,1)}, u32[]{:S(2)}, u32[]{:S(2)}) collective-permute-start(bf16[4,128,128]{2,1,0:T(8,128)(2,1)} %fusion.25), channel_id=1, source_target_pairs={{0,64},{4,68},{8,72},{12,76},{16,80},{20,84},{24,88},{28,92},{32,9... | collective-permute-start | bytes 393224 | tf_op jit(solution)/shard_map/ppermute | solution.py:11
  117.4 1.6 %add_convert_fusion.1 = bf16[4,128,1024]{2,1,0:T(8,128)(2,1)} fusion(f32[4,128,1024]{2,1,0:T(8,128)S(1)} %fusion.41, bf16[1024,4,128]{0,2,1:T(8,128)(2,1)S(1)} %bitcast.54, bf16[4,128,128]{2,1,0:T(8,128)(2,1)S(1)} %collective-permute-done, bf16[4,128,128]{2,1,0:T(8,128)(2,1)S(1)} %collective-permute-done.1, ...), kind=kOutput, calls=%fused_computation.10 | convolution fusion | flops 136577024 | bytes 4849749 | tf_op jit(solution)/shard_map/the,hde->thd/dot_general | solution.py:68
  119.0 2.3 %copy.25 = bf16[1024,512]{1,0:T(8,128)(2,1)} copy(bf16[1024,512]{0,1:T(8,128)(2,1)} %bitcast.71) | data formatting | bytes 2097152
  121.3 3.7 %add_convert_fusion = bf16[4,128,1024]{2,1,0:T(8,128)(2,1)} fusion(f32[4,128,1024]{2,1,0:T(8,128)} %fusion.42, bf16[1024,4,128]{0,2,1:T(8,128)(2,1)} %bitcast.67, bf16[4,128,128]{2,1,0:T(8,128)(2,1)S(1)} %collective-permute-done.5, bf16[4,128,128]{2,1,0:T(8,128)(2,1)} %copy-done.3, bf16[4,128,128]{2,1,0:T(8,128)(2,1)} %copy-done.6, ...), kind=kOutput, calls=%fused_computation.9 | convolution fusion | flops 136577024 | bytes 4849749 | tf_op jit(solution)/shard_map/the,hde->thd/dot_general | solution.py:72
  125.0 2.3 %copy.26 = bf16[1024,512]{1,0:T(8,128)(2,1)} copy(bf16[1024,512]{0,1:T(8,128)(2,1)} %bitcast.70) | data formatting | bytes 2097152
  127.3 1.7 %fusion.35 = f32[4,128,1024]{2,1,0:T(8,128)S(1)} fusion(bf16[1024,4,128]{0,2,1:T(8,128)(2,1)S(1)} %bitcast.59, bf16[4,128,128]{2,1,0:T(8,128)(2,1)S(1)} %collective-permute-done.5, bf16[4,128,128]{2,1,0:T(8,128)(2,1)} %copy-done.3, bf16[4,128,128]{2,1,0:T(8,128)(2,1)} %copy-done.6, bf16[4,128,128]{2,1,0:T(8,128)(2,1)} %copy-done.9, ...), kind=kOutput, calls=%fused_computation.63 | convolution fusion | flops 135528448 | bytes 3801173 | tf_op jit(solution)/shard_map/thd,hde->the/dot_general | solution.py:76
  129.0 4.8 %fusion.5 = bf16[1024,4,128]{0,2,1:T(8,128)(2,1)S(1)} fusion(f32[4,128,1024]{2,1,0:T(8,128)S(1)} %fusion.35, bf16[1024,4,128]{0,2,1:T(8,128)(2,1)S(1)} %bitcast.55, bf16[4,1024,1024]{2,1,0:T(8,128)(2,1)} %copy-done), kind=kOutput, calls=%fused_computation.8 | convolution fusion | flops 1074790400 | bytes 12582912 | tf_op jit(solution)/shard_map/hts,the->she/dot_general | solution.py:75
  (58 shorter events, 11.9 us)
Async XLA Ops:
  7.2 53.2 %all-gather.2.cloned.1.call-start = ((), (), s32[]{:S(2)}) async-start(), calls=%async_computation | async-start | bytes 5242880 | tf_op jit(solution)/shard_map/all_gather | solution.py:21
  71.0 13.3 %copy-start.1 = (bf16[1,1024,512]{1,2,0:T(8,128)(2,1)}, bf16[1,1024,512]{1,2,0:T(8,128)(2,1)S(1)}, u32[]{:S(2)}) copy-start(bf16[1,1024,512]{1,2,0:T(8,128)(2,1)S(1)} %get-tuple-element.16) | copy-start | bytes 3145732
  83.7 6.5 %copy-start = (bf16[4,1024,1024]{2,1,0:T(8,128)(2,1)}, bf16[4,1024,1024]{2,1,0:T(8,128)(2,1)S(1)}, u32[]{:S(2)}) copy-start(bf16[4,1024,1024]{2,1,0:T(8,128)(2,1)S(1)} %select_convert_fusion) | copy-start | bytes 25165828
  83.7 4.9 %collective-permute-start = (bf16[4,128,128]{2,1,0:T(8,128)(2,1)S(1)}, bf16[4,128,128]{2,1,0:T(8,128)(2,1)S(1)}, u32[]{:S(2)}, u32[]{:S(2)}) collective-permute-start(bf16[4,128,128]{2,1,0:T(8,128)(2,1)S(1)} %get-tuple-element.17), channel_id=1, source_target_pairs={{0,4},{4,0},{8,12},{12,8},{16,20},{20,16},{24,28},{28,24},{32,36},... | collective-permute-start | bytes 393224 | tf_op jit(solution)/shard_map/ppermute | solution.py:11
  83.8 33.6 %copy-start.13 = (f32[4]{0:T(128)S(1)}, f32[4]{0:T(128)}, u32[]{:S(2)}) copy-start(f32[4]{0:T(128)} %get-tuple-element.13) | copy-start | bytes 52
  83.8 6.4 %collective-permute-start.5 = (bf16[4,128,128]{2,1,0:T(8,128)(2,1)S(1)}, bf16[4,128,128]{2,1,0:T(8,128)(2,1)S(1)}, u32[]{:S(2)}, u32[]{:S(2)}) collective-permute-start(bf16[4,128,128]{2,1,0:T(8,128)(2,1)S(1)} %get-tuple-element.19), channel_id=1, source_target_pairs={{0,4},{4,0},{8,12},{12,8},{16,20},{20,16},{24,28},{28,24},{32,36},... | collective-permute-start | bytes 393224 | tf_op jit(solution)/shard_map/ppermute | solution.py:11
  88.6 6.5 %collective-permute-start.1 = (bf16[4,128,128]{2,1,0:T(8,128)(2,1)S(1)}, bf16[4,128,128]{2,1,0:T(8,128)(2,1)S(1)}, u32[]{:S(2)}, u32[]{:S(2)}) collective-permute-start(bf16[4,128,128]{2,1,0:T(8,128)(2,1)S(1)} %fusion.26), channel_id=1, source_target_pairs={{0,8},{4,12},{8,0},{12,4},{16,24},{20,28},{24,16},{28,20},{32,40},... | collective-permute-start | bytes 393224 | tf_op jit(solution)/shard_map/ppermute | solution.py:11
  90.2 8.0 %collective-permute-start.6 = (bf16[4,128,128]{2,1,0:T(8,128)(2,1)S(1)}, bf16[4,128,128]{2,1,0:T(8,128)(2,1)S(1)}, u32[]{:S(2)}, u32[]{:S(2)}) collective-permute-start(bf16[4,128,128]{2,1,0:T(8,128)(2,1)S(1)} %fusion.28), channel_id=1, source_target_pairs={{0,8},{4,12},{8,0},{12,4},{16,24},{20,28},{24,16},{28,20},{32,40},... | collective-permute-start | bytes 393224 | tf_op jit(solution)/shard_map/ppermute | solution.py:11
  95.1 8.0 %collective-permute-start.2 = (bf16[4,128,128]{2,1,0:T(8,128)(2,1)S(1)}, bf16[4,128,128]{2,1,0:T(8,128)(2,1)S(1)}, u32[]{:S(2)}, u32[]{:S(2)}) collective-permute-start(bf16[4,128,128]{2,1,0:T(8,128)(2,1)S(1)} %fusion.30), channel_id=1, source_target_pairs={{0,16},{4,20},{8,24},{12,28},{16,0},{20,4},{24,8},{28,12},{32,48},... | collective-permute-start | bytes 393224 | tf_op jit(solution)/shard_map/ppermute | solution.py:11
  98.2 20.8 %copy-start.3 = (bf16[4,128,128]{2,1,0:T(8,128)(2,1)}, bf16[4,128,128]{2,1,0:T(8,128)(2,1)S(1)}, u32[]{:S(2)}) copy-start(bf16[4,128,128]{2,1,0:T(8,128)(2,1)S(1)} %collective-permute-done.6) | copy-start | bytes 393220
  98.2 6.7 %collective-permute-start.7 = (bf16[4,128,128]{2,1,0:T(8,128)(2,1)S(1)}, bf16[4,128,128]{2,1,0:T(8,128)(2,1)S(1)}, u32[]{:S(2)}, u32[]{:S(2)}) collective-permute-start(bf16[4,128,128]{2,1,0:T(8,128)(2,1)S(1)} %fusion.31), channel_id=1, source_target_pairs={{0,16},{4,20},{8,24},{12,28},{16,0},{20,4},{24,8},{28,12},{32,48},... | collective-permute-start | bytes 393224 | tf_op jit(solution)/shard_map/ppermute | solution.py:11
  103.1 15.9 %copy-start.4 = (bf16[4,128,128]{2,1,0:T(8,128)(2,1)}, bf16[4,128,128]{2,1,0:T(8,128)(2,1)S(1)}, u32[]{:S(2)}) copy-start(bf16[4,128,128]{2,1,0:T(8,128)(2,1)S(1)} %collective-permute-done.2) | copy-start | bytes 393220
  103.2 6.2 %collective-permute-start.3 = (bf16[4,128,128]{2,1,0:T(8,128)(2,1)S(1)}, bf16[4,128,128]{2,1,0:T(8,128)(2,1)S(1)}, u32[]{:S(2)}, u32[]{:S(2)}) collective-permute-start(bf16[4,128,128]{2,1,0:T(8,128)(2,1)S(1)} %fusion.27), channel_id=1, source_target_pairs={{0,32},{4,36},{8,40},{12,44},{16,48},{20,52},{24,56},{28,60},{32,0... | collective-permute-start | bytes 393224 | tf_op jit(solution)/shard_map/ppermute | solution.py:11
  105.0 14.0 %copy-start.6 = (bf16[4,128,128]{2,1,0:T(8,128)(2,1)}, bf16[4,128,128]{2,1,0:T(8,128)(2,1)S(1)}, u32[]{:S(2)}) copy-start(bf16[4,128,128]{2,1,0:T(8,128)(2,1)S(1)} %collective-permute-done.7) | copy-start | bytes 393220
  105.0 7.9 %collective-permute-start.8 = (bf16[4,128,128]{2,1,0:T(8,128)(2,1)S(1)}, bf16[4,128,128]{2,1,0:T(8,128)(2,1)S(1)}, u32[]{:S(2)}, u32[]{:S(2)}) collective-permute-start(bf16[4,128,128]{2,1,0:T(8,128)(2,1)S(1)} %fusion.29), channel_id=1, source_target_pairs={{0,32},{4,36},{8,40},{12,44},{16,48},{20,52},{24,56},{28,60},{32,0... | collective-permute-start | bytes 393224 | tf_op jit(solution)/shard_map/ppermute | solution.py:11
  109.4 9.6 %copy-start.7 = (bf16[4,128,128]{2,1,0:T(8,128)(2,1)}, bf16[4,128,128]{2,1,0:T(8,128)(2,1)S(1)}, u32[]{:S(2)}) copy-start(bf16[4,128,128]{2,1,0:T(8,128)(2,1)S(1)} %collective-permute-done.3) | copy-start | bytes 393220
  109.5 7.9 %collective-permute-start.4 = (bf16[4,128,128]{2,1,0:T(8,128)(2,1)S(1)}, bf16[4,128,128]{2,1,0:T(8,128)(2,1)S(1)}, u32[]{:S(2)}, u32[]{:S(2)}) collective-permute-start(bf16[4,128,128]{2,1,0:T(8,128)(2,1)S(1)} %fusion.15), channel_id=1, source_target_pairs={{0,64},{4,68},{8,72},{12,76},{16,80},{20,84},{24,88},{28,92},{32,9... | collective-permute-start | bytes 393224 | tf_op jit(solution)/shard_map/ppermute | solution.py:11
  112.9 6.1 %copy-start.9 = (bf16[4,128,128]{2,1,0:T(8,128)(2,1)}, bf16[4,128,128]{2,1,0:T(8,128)(2,1)S(1)}, u32[]{:S(2)}) copy-start(bf16[4,128,128]{2,1,0:T(8,128)(2,1)S(1)} %collective-permute-done.8) | copy-start | bytes 393220
  113.7 7.6 %collective-permute-start.9 = (bf16[4,128,128]{2,1,0:T(8,128)(2,1)}, bf16[4,128,128]{2,1,0:T(8,128)(2,1)}, u32[]{:S(2)}, u32[]{:S(2)}) collective-permute-start(bf16[4,128,128]{2,1,0:T(8,128)(2,1)} %fusion.25), channel_id=1, source_target_pairs={{0,64},{4,68},{8,72},{12,76},{16,80},{20,84},{24,88},{28,92},{32,9... | collective-permute-start | bytes 393224 | tf_op jit(solution)/shard_map/ppermute | solution.py:11
  129.0 4.9 %copy-start.2 = (f32[4,128,1024]{2,1,0:T(8,128)S(1)}, f32[4,128,1024]{2,1,0:T(8,128)}, u32[]{:S(2)}) copy-start(f32[4,128,1024]{2,1,0:T(8,128)} %fusion.40) | copy-start | bytes 6291460
  129.0 4.9 %copy-start.5 = (bf16[4,128,128]{2,1,0:T(8,128)(2,1)S(1)}, bf16[4,128,128]{2,1,0:T(8,128)(2,1)}, u32[]{:S(2)}) copy-start(bf16[4,128,128]{2,1,0:T(8,128)(2,1)} %copy-done.4) | copy-start | bytes 393220
  129.0 4.9 %copy-start.8 = (bf16[4,128,128]{2,1,0:T(8,128)(2,1)S(1)}, bf16[4,128,128]{2,1,0:T(8,128)(2,1)}, u32[]{:S(2)}) copy-start(bf16[4,128,128]{2,1,0:T(8,128)(2,1)} %copy-done.7) | copy-start | bytes 393220
  129.0 4.9 %copy-start.12 = (bf16[4,128,128]{2,1,0:T(8,128)(2,1)S(1)}, bf16[4,128,128]{2,1,0:T(8,128)(2,1)}, u32[]{:S(2)}) copy-start(bf16[4,128,128]{2,1,0:T(8,128)(2,1)} %copy-done.11) | copy-start | bytes 393220
  129.0 4.9 %copy-start.14 = (f32[4]{0:T(128)S(1)}, f32[4]{0:T(128)}, u32[]{:S(2)}) copy-start(f32[4]{0:T(128)} %get-tuple-element.13) | copy-start | bytes 52
  (2 other events, 2.8 us)
Sparse Core Ops, SparseCore 0:
  9.6 50.7 all-gather.1
where the time goes:
time: 144 us
  waiting for transfers between devices  60 us (42%)
  matrix products  39.6 us (28%)
  starting transfers between devices  17.1 us (12%)
  between operations  14.3 us (10%)
  local copies, waits for them, and re-layouts  9.05 us (6%)
  other arithmetic  4.03 us (3%)
    all_gather x1, waiting for transfers between devices, per_device(): lax.all_gather(inputs, 'head', axis=1, tiled=True)  48.1 us
    ppermute x10, starting transfers between devices, partner(): return lax.ppermute(value, axis, pairs)  17 us
    ppermute x10, waiting for transfers between devices, partner(): return lax.ppermute(value, axis, pairs)  11.2 us
    dot_general x1, matrix products, per_device(): jnp.einsum('tn,jnf->jtf', lax.all_gather(inputs, 'head', axis=1, tiled=Tr...  10.3 us
    unnamed x34, local copies, waits for them, and re-layouts  7.26 us
    dot_general x1, matrix products, per_device(): jnp.einsum('hts,the->she', attend, grad_rows, preferred_element_type=jnp....  4.81 us
    dot_general x1, matrix products, per_device(): jnp.einsum('hts,she->the', attend, values, preferred_element_type=jnp.flo...  4.29 us
    dot_general x1, matrix products, per_device(): jnp.einsum('the,hde->thd', values, backward_low, preferred_element_type=j...  3.73 us
  transfers between devices with their start and end apart: 11, of which 6 were waited for; matrix products, arithmetic and copies ran while one was open for 9% of the time, Pallas kernels for 0%

commit v1 on v0

--- a/solution.py
+++ b/solution.py
@@ -16,11 +16,17 @@
     head_count = level_weight.shape[0]
     width = w_qkv.shape[2]
     head_size = width // head_count
+    raise_sources_all = lambda vals: jnp.concatenate(
+        lax.all_to_all(
+            jnp.stack([vals for _ in range(lax.psum(1, axis_name="head"))], axis=0),
+            axis_name="head",
+            split_axis=0,
+            concat_axis=0,
+        ),
+        axis=1,
+    )
     projected = jnp.einsum(
-        "tn,jnf->jtf",
-        lax.all_gather(inputs, "head", axis=1, tiled=True),
-        w_qkv,
-        preferred_element_type=jnp.float32,
+        "tn,jnf->jtf", raise_sources_all(inputs), w_qkv, preferred_element_type=jnp.float32
     ).astype(jnp.bfloat16)
     queries = projected[0].reshape(rows, head_count, head_size)
     keys = projected[1].reshape(rows, head_count, head_size)

time: 144 us -> 151 us (1.049)
  local copies, waits for them, and re-layouts: 9.05 us -> 26.8 us
  between operations: 14.3 us -> 0.88 us
  starting transfers between devices: 17.1 us -> 23.7 us
  waiting for transfers between devices: 60 us -> 57.9 us
    all_gather x1 -> x0, waiting for transfers between devices: 48.1 us -> none  [per_device(): lax.all_gather(inputs, 'head', axis=1, tiled=True)]
    all_to_all x0 -> x1, waiting for transfers between devices: none -> 46.5 us  [per_device(): lax.all_to_all(jnp.stack([vals for _ in range(lax.psum(1, axis_name='head...]
    reshape x0 -> x2, local copies, waits for them, and re-layouts: none -> 15.1 us  [per_device(): jnp.concatenate(lax.all_to_all(jnp.stack([vals for _ in range(lax.psum(1,...]
    all_to_all x0 -> x1, starting transfers between devices: none -> 4.97 us  [per_device(): lax.all_to_all(jnp.stack([vals for _ in range(lax.psum(1, axis_name='head...]
    another operation x0 -> x1, local copies, waits for them, and re-layouts: none -> 3.53 us  [per_device(): jnp.stack([vals for _ in range(lax.psum(1, axis_name='head'))], axis=0)]
    dot_general x1, matrix products: 4.81 us -> 2.37 us  [per_device(): jnp.einsum('hts,the->she', attend, grad_rows, preferred_element_type=jnp....]
    ppermute x10, starting transfers between devices: 17 us -> 18.7 us  [partner(): return lax.ppermute(value, axis, pairs)]
  transfers between devices with their start and end apart: 11 -> 11, of which waited for: 6 -> 5; matrix products, arithmetic and copies ran while one was open for 9% -> 6% of each run, Pallas kernels for 0% -> 0%
where the time goes in v1:
time: 151 us
  waiting for transfers between devices  57.9 us (38%)
  matrix products  39.1 us (26%)
  local copies, waits for them, and re-layouts  26.8 us (18%)
  starting transfers between devices  23.7 us (16%)
  other arithmetic  2.53 us (2%)
    all_to_all x1, waiting for transfers between devices, per_device(): lax.all_to_all(jnp.stack([vals for _ in range(lax.psum(1, axis_name='head...  46.5 us
    ppermute x10, starting transfers between devices, partner(): return lax.ppermute(value, axis, pairs)  18.7 us
    reshape x2, local copies, waits for them, and re-layouts, per_device(): jnp.concatenate(lax.all_to_all(jnp.stack([vals for _ in range(lax.psum(1,...  15.1 us
    ppermute x10, waiting for transfers between devices, partner(): return lax.ppermute(value, axis, pairs)  11.4 us
    dot_general x1, matrix products, per_device(): jnp.einsum('tn,jnf->jtf', raise_sources_all(inputs), w_qkv, preferred_ele...  10.3 us
    unnamed x34, local copies, waits for them, and re-layouts  7.26 us
    all_to_all x1, starting transfers between devices, per_device(): lax.all_to_all(jnp.stack([vals for _ in range(lax.psum(1, axis_name='head...  4.97 us
    dot_general x1, matrix products, per_device(): jnp.einsum('the,she->hts', grad_rows, values, preferred_element_type=jnp....  4.28 us
  transfers between devices with their start and end apart: 11, of which 5 were waited for; matrix products, arithmetic and copies ran while one was open for 6% of the time, Pallas kernels for 0%

profile of v1, /device:TPU:0, one launch (start us, length us, event | category | flops | bytes accessed | tf_op | source)
XLA Modules:
  0.0 150.9 jit_solution(5113017982983519478)
XLA Ops:
  0.6 3.5 %stack.2 = bf16[4,1024,512]{2,1,0:T(8,128)(2,1)} broadcast(bf16[1024,512]{1,0:T(8,128)(2,1)} %param.4), dimensions={1,2} | broadcast | bytes 5242880 | tf_op jit(solution)/shard_map/stack | solution.py:21
  4.2 5.0 %all-to-all-start = ((bf16[4,1024,512]{2,1,0:T(8,128)(2,1)}), bf16[4,1024,512]{2,1,0:T(8,128)(2,1)}, u32[]{:S(2)}, u32[]{:S(2)}) async-start(bf16[4,1024,512]{2,1,0:T(8,128)(2,1)} %stack.2), calls=%async_computation | async-start | bytes 8388608 | tf_op jit(solution)/shard_map/all_to_all | solution.py:20
  11.8 46.5 %all-to-all-done = bf16[4,1024,512]{2,1,0:T(8,128)(2,1)} async-done(((bf16[4,1024,512]{2,1,0:T(8,128)(2,1)}), bf16[4,1024,512]{2,1,0:T(8,128)(2,1)}, u32[]{:S(2)}, u32[]{:S(2)}) %all-to-all-start) | async-done | bytes 4194336 | tf_op jit(solution)/shard_map/all_to_all | solution.py:20
  58.3 7.4 %copy.28 = bf16[1024,4,512]{2,1,0:T(4,128)(2,1)} copy(bf16[1024,4,512]{2,0,1:T(8,128)(2,1)} %bitcast) | data formatting | bytes 8388608 | tf_op jit(solution)/shard_map/reshape | solution.py:19
  65.7 7.7 %reshape.84 = bf16[1024,2048,1]{1,0,2:T(8,128)(2,1)} reshape(bf16[1024,4,512]{2,1,0:T(4,128)(2,1)} %copy.28) | data formatting | bytes 8388608 | tf_op jit(solution)/shard_map/reshape | solution.py:19
  73.5 10.3 %convert_bitcast_fusion = bf16[3,1024,512]{1,2,0:T(8,128)(2,1)S(1)} fusion(bf16[3,2048,512]{2,1,0:T(8,128)(2,1)} %param.5, bf16[1024,2048,1]{1,0,2:T(8,128)(2,1)} %reshape.84), kind=kOutput, calls=%fused_computation.4 | convolution fusion | flops 6444023808 | bytes 13631488 | tf_op jit(solution)/shard_map/tn,jnf->jtf/dot_general | solution.py:28
  86.4 3.1 %select_convert_fusion = bf16[4,1024,1024]{2,1,0:T(8,128)(2,1)S(1)} fusion(bf16[1024,4,128]{0,2,1:T(8,128)(2,1)S(1)} %bitcast.62, bf16[1024,4,128]{0,2,1:T(8,128)(2,1)S(1)} %bitcast.54, f32[4]{0:T(128)S(1)} %get-tuple-element.15, pred[1024,1024]{1,0:T(8,128)(4,1)S(1)} %copy-done.8), kind=kOutput, calls=%fused_computation.2 | convolution fusion | flops 1086324736 | bytes 11534352 | tf_op jit(solution)/shard_map/thd,shd->hts/dot_general | solution.py:65
  89.5 4.3 %fusion = bf16[4,1024,1024]{2,1,0:T(8,128)(2,1)S(1)} fusion(bf16[1024,4,128]{0,2,1:T(8,128)(2,1)S(1)} %bitcast.50, bf16[1024,4,128]{0,2,1:T(8,128)(2,1)S(1)} %bitcast.58, f32[4]{0:T(128)S(1)} %get-tuple-element.15, pred[1024,1024]{1,0:T(8,128)(4,1)} %iota_compare_fusion), kind=kOutput, calls=%fused_computation.1 | convolution fusion | flops 1086324736 | bytes 11534352 | tf_op jit(solution)/shard_map/the,she->hts/dot_general | solution.py:67
  93.8 2.6 %fusion.38 = f32[4,128,1024]{2,1,0:T(8,128)} fusion(bf16[1024,4,128]{0,2,1:T(8,128)(2,1)S(1)} %bitcast.63, bf16[4,1024,1024]{2,1,0:T(8,128)(2,1)S(1)} %fusion), kind=kOutput, calls=%fused_computation.64 | convolution fusion | flops 1073741824 | bytes 11534336 | tf_op jit(solution)/shard_map/hts,thd->shd/dot_general | solution.py:77
  96.4 4.2 %fusion.37 = f32[4,128,1024]{2,1,0:T(8,128)} fusion(bf16[1024,4,128]{0,2,1:T(8,128)(2,1)S(1)} %bitcast.55, bf16[4,1024,1024]{2,1,0:T(8,128)(2,1)S(1)} %fusion), kind=kOutput, calls=%fused_computation.63 | convolution fusion | flops 1073741824 | bytes 11534336 | tf_op jit(solution)/shard_map/hts,shd->thd/dot_general | solution.py:73
  101.2 2.9 %fusion.36 = f32[4,128,1024]{2,1,0:T(8,128)S(1)} fusion(bf16[1024,4,128]{0,2,1:T(8,128)(2,1)S(1)} %bitcast.59, bf16[4,1024,1024]{2,1,0:T(8,128)(2,1)S(1)} %select_convert_fusion), kind=kOutput, calls=%fused_computation.62 | convolution fusion | flops 1073741824 | bytes 11534336 | tf_op jit(solution)/shard_map/hts,she->the/dot_general | solution.py:69
  106.4 4.2 %collective-permute-done.6 = bf16[4,128,128]{2,1,0:T(8,128)(2,1)S(1)} collective-permute-done((bf16[4,128,128]{2,1,0:T(8,128)(2,1)S(1)}, bf16[4,128,128]{2,1,0:T(8,128)(2,1)S(1)}, u32[]{:S(2)}, u32[]{:S(2)}) %collective-permute-start.6) | collective-permute-done | bytes 131104 | tf_op jit(solution)/shard_map/ppermute | solution.py:11
  110.7 3.1 %collective-permute-start.7 = (bf16[4,128,128]{2,1,0:T(8,128)(2,1)S(1)}, bf16[4,128,128]{2,1,0:T(8,128)(2,1)S(1)}, u32[]{:S(2)}, u32[]{:S(2)}) collective-permute-start(bf16[4,128,128]{2,1,0:T(8,128)(2,1)S(1)} %fusion.27), channel_id=1, source_target_pairs={{0,16},{4,20},{8,24},{12,28},{16,0},{20,4},{24,8},{28,12},{32,48},... | collective-permute-start | bytes 393224 | tf_op jit(solution)/shard_map/ppermute | solution.py:11
  113.9 2.1 %collective-permute-start.2 = (bf16[4,128,128]{2,1,0:T(8,128)(2,1)S(1)}, bf16[4,128,128]{2,1,0:T(8,128)(2,1)S(1)}, u32[]{:S(2)}, u32[]{:S(2)}) collective-permute-start(bf16[4,128,128]{2,1,0:T(8,128)(2,1)S(1)} %fusion.26), channel_id=1, source_target_pairs={{0,16},{4,20},{8,24},{12,28},{16,0},{20,4},{24,8},{28,12},{32,48},... | collective-permute-start | bytes 393224 | tf_op jit(solution)/shard_map/ppermute | solution.py:11
  116.0 2.6 %collective-permute-done.7 = bf16[4,128,128]{2,1,0:T(8,128)(2,1)S(1)} collective-permute-done((bf16[4,128,128]{2,1,0:T(8,128)(2,1)S(1)}, bf16[4,128,128]{2,1,0:T(8,128)(2,1)S(1)}, u32[]{:S(2)}, u32[]{:S(2)}) %collective-permute-start.7) | collective-permute-done | bytes 131104 | tf_op jit(solution)/shard_map/ppermute | solution.py:11
  122.7 2.3 %collective-permute-done.8 = bf16[4,128,128]{2,1,0:T(8,128)(2,1)S(1)} collective-permute-done((bf16[4,128,128]{2,1,0:T(8,128)(2,1)S(1)}, bf16[4,128,128]{2,1,0:T(8,128)(2,1)S(1)}, u32[]{:S(2)}, u32[]{:S(2)}) %collective-permute-start.8) | collective-permute-done | bytes 131104 | tf_op jit(solution)/shard_map/ppermute | solution.py:11
  125.1 4.2 %collective-permute-start.9 = (bf16[4,128,128]{2,1,0:T(8,128)(2,1)S(1)}, bf16[4,128,128]{2,1,0:T(8,128)(2,1)S(1)}, u32[]{:S(2)}, u32[]{:S(2)}) collective-permute-start(bf16[4,128,128]{2,1,0:T(8,128)(2,1)S(1)} %fusion.21), channel_id=1, source_target_pairs={{0,64},{4,68},{8,72},{12,76},{16,80},{20,84},{24,88},{28,92},{32,9... | collective-permute-start | bytes 393224 | tf_op jit(solution)/shard_map/ppermute | solution.py:11
  129.4 2.7 %collective-permute-start.4 = (bf16[4,128,128]{2,1,0:T(8,128)(2,1)S(1)}, bf16[4,128,128]{2,1,0:T(8,128)(2,1)S(1)}, u32[]{:S(2)}, u32[]{:S(2)}) collective-permute-start(bf16[4,128,128]{2,1,0:T(8,128)(2,1)S(1)} %fusion.11), channel_id=1, source_target_pairs={{0,64},{4,68},{8,72},{12,76},{16,80},{20,84},{24,88},{28,92},{32,9... | collective-permute-start | bytes 393224 | tf_op jit(solution)/shard_map/ppermute | solution.py:11
  132.0 2.2 %collective-permute-done.9 = bf16[4,128,128]{2,1,0:T(8,128)(2,1)S(1)} collective-permute-done((bf16[4,128,128]{2,1,0:T(8,128)(2,1)S(1)}, bf16[4,128,128]{2,1,0:T(8,128)(2,1)S(1)}, u32[]{:S(2)}, u32[]{:S(2)}) %collective-permute-start.9) | collective-permute-done | bytes 131104 | tf_op jit(solution)/shard_map/ppermute | solution.py:11
  134.9 2.4 %fusion.1 = bf16[1024,4,128]{0,2,1:T(8,128)(2,1)} fusion(f32[4,128,1024]{2,1,0:T(8,128)S(1)} %fusion.31, bf16[1024,4,128]{0,2,1:T(8,128)(2,1)S(1)} %bitcast.51, bf16[4,1024,1024]{2,1,0:T(8,128)(2,1)S(1)} %select_convert_fusion), kind=kOutput, calls=%fused_computation.6 | convolution fusion | flops 1074790400 | bytes 12582912 | tf_op jit(solution)/shard_map/hts,the->she/dot_general | solution.py:81
  138.9 2.3 %copy.45 = bf16[1024,512]{1,0:T(8,128)(2,1)} copy(bf16[1024,512]{0,1:T(8,128)(2,1)} %bitcast.68) | data formatting | bytes 2097152
  141.1 2.3 %copy.48 = bf16[1024,512]{1,0:T(8,128)(2,1)} copy(bf16[1024,512]{0,1:T(8,128)(2,1)} %bitcast.65) | data formatting | bytes 2097152
  143.4 2.4 %add_convert_fusion = bf16[4,128,1024]{2,1,0:T(8,128)(2,1)S(1)} fusion(f32[4,128,1024]{2,1,0:T(8,128)} %fusion.38, bf16[1024,4,128]{0,2,1:T(8,128)(2,1)S(1)} %bitcast.60, bf16[4,128,128]{2,1,0:T(8,128)(2,1)S(1)} %collective-permute-done.5, bf16[4,128,128]{2,1,0:T(8,128)(2,1)} %copy-done.2, bf16[4,128,128]{2,1,0:T(8,128)(2,1)} %copy-done.4, ...), kind=kOutput, calls=%fused_computation.7 | convolution fusion | flops 136577024 | bytes 4849749 | tf_op jit(solution)/shard_map/the,hde->thd/dot_general | solution.py:78
  147.2 2.4 %add_convert_fusion.1 = bf16[4,128,1024]{2,1,0:T(8,128)(2,1)S(1)} fusion(f32[4,128,1024]{2,1,0:T(8,128)} %fusion.37, bf16[1024,4,128]{0,2,1:T(8,128)(2,1)S(1)} %bitcast.52, bf16[4,128,128]{2,1,0:T(8,128)(2,1)S(1)} %collective-permute-done, bf16[4,128,128]{2,1,0:T(8,128)(2,1)S(1)} %collective-permute-done.1, bf16[4,128,128]{2,1,0:T(8,128)(2,1)} %copy-done.3, ...), kind=kOutput, calls=%fused_computation.8 | convolution fusion | flops 136577024 | bytes 4849749 | tf_op jit(solution)/shard_map/the,hde->thd/dot_general | solution.py:74
  (60 shorter events, 17.3 us)
Async XLA Ops:
  4.2 5.0 %copy-start.7 = (bf16[1024,512]{1,0:T(8,128)(2,1)S(1)}, bf16[1024,512]{1,0:T(8,128)(2,1)}, u32[]{:S(2)}) copy-start(bf16[1024,512]{1,0:T(8,128)(2,1)} %param.7) | copy-start | bytes 3145732
  4.2 5.5 %copy-start.13 = (f32[4,6]{1,0:T(4,128)S(1)}, f32[4,6]{1,0:T(4,128)}, u32[]{:S(2)}) copy-start(f32[4,6]{1,0:T(4,128)} %param.6) | copy-start | bytes 292
  4.2 54.2 %all-to-all-start = ((bf16[4,1024,512]{2,1,0:T(8,128)(2,1)}), bf16[4,1024,512]{2,1,0:T(8,128)(2,1)}, u32[]{:S(2)}, u32[]{:S(2)}) async-start(bf16[4,1024,512]{2,1,0:T(8,128)(2,1)} %stack.2), calls=%async_computation | async-start | bytes 8388608 | tf_op jit(solution)/shard_map/all_to_all | solution.py:20
  96.4 4.2 %copy-start.12 = (bf16[4,128,128]{2,1,0:T(8,128)(2,1)S(1)}, bf16[4,128,128]{2,1,0:T(8,128)(2,1)}, u32[]{:S(2)}) copy-start(bf16[4,128,128]{2,1,0:T(8,128)(2,1)} %get-tuple-element.23) | copy-start | bytes 393220
  96.4 4.2 %copy-start.11 = (bf16[4,128,128]{2,1,0:T(8,128)(2,1)S(1)}, bf16[4,128,128]{2,1,0:T(8,128)(2,1)}, u32[]{:S(2)}) copy-start(bf16[4,128,128]{2,1,0:T(8,128)(2,1)} %get-tuple-element.21) | copy-start | bytes 393220
  100.7 3.4 %collective-permute-start.5 = (bf16[4,128,128]{2,1,0:T(8,128)(2,1)S(1)}, bf16[4,128,128]{2,1,0:T(8,128)(2,1)S(1)}, u32[]{:S(2)}, u32[]{:S(2)}) collective-permute-start(bf16[4,128,128]{2,1,0:T(8,128)(2,1)S(1)} %copy-done.12), channel_id=1, source_target_pairs={{0,4},{4,0},{8,12},{12,8},{16,20},{20,16},{24,28},{28,24},{32,36},... | collective-permute-start | bytes 393224 | tf_op jit(solution)/shard_map/ppermute | solution.py:11
  100.7 3.4 %copy-start.1 = (f32[4,128,128]{2,1,0:T(8,128)S(1)}, f32[4,128,128]{2,1,0:T(8,128)}, u32[]{:S(2)}) copy-start(f32[4,128,128]{2,1,0:T(8,128)} %get-tuple-element.24) | copy-start | bytes 786436
  100.7 5.1 %copy-start = (f32[4,128,128]{2,1,0:T(8,128)S(1)}, f32[4,128,128]{2,1,0:T(8,128)}, u32[]{:S(2)}) copy-start(f32[4,128,128]{2,1,0:T(8,128)} %get-tuple-element.22) | copy-start | bytes 786436
  100.7 5.1 %collective-permute-start = (bf16[4,128,128]{2,1,0:T(8,128)(2,1)S(1)}, bf16[4,128,128]{2,1,0:T(8,128)(2,1)S(1)}, u32[]{:S(2)}, u32[]{:S(2)}) collective-permute-start(bf16[4,128,128]{2,1,0:T(8,128)(2,1)S(1)} %copy-done.11), channel_id=1, source_target_pairs={{0,4},{4,0},{8,12},{12,8},{16,20},{20,16},{24,28},{28,24},{32,36},... | collective-permute-start | bytes 393224 | tf_op jit(solution)/shard_map/ppermute | solution.py:11
  104.1 30.1 %copy-start.14 = (f32[4]{0:T(128)S(1)}, f32[4]{0:T(128)}, u32[]{:S(2)}) copy-start(f32[4]{0:T(128)} %get-tuple-element.17) | copy-start | bytes 52
  104.2 6.4 %collective-permute-start.6 = (bf16[4,128,128]{2,1,0:T(8,128)(2,1)S(1)}, bf16[4,128,128]{2,1,0:T(8,128)(2,1)S(1)}, u32[]{:S(2)}, u32[]{:S(2)}) collective-permute-start(bf16[4,128,128]{2,1,0:T(8,128)(2,1)S(1)} %fusion.24), channel_id=1, source_target_pairs={{0,8},{4,12},{8,0},{12,4},{16,24},{20,28},{24,16},{28,20},{32,40},... | collective-permute-start | bytes 393224 | tf_op jit(solution)/shard_map/ppermute | solution.py:11
  105.8 8.0 %collective-permute-start.1 = (bf16[4,128,128]{2,1,0:T(8,128)(2,1)S(1)}, bf16[4,128,128]{2,1,0:T(8,128)(2,1)S(1)}, u32[]{:S(2)}, u32[]{:S(2)}) collective-permute-start(bf16[4,128,128]{2,1,0:T(8,128)(2,1)S(1)} %fusion.22), channel_id=1, source_target_pairs={{0,8},{4,12},{8,0},{12,4},{16,24},{20,28},{24,16},{28,20},{32,40},... | collective-permute-start | bytes 393224 | tf_op jit(solution)/shard_map/ppermute | solution.py:11
  110.6 24.2 %copy-start.2 = (bf16[4,128,128]{2,1,0:T(8,128)(2,1)}, bf16[4,128,128]{2,1,0:T(8,128)(2,1)S(1)}, u32[]{:S(2)}) copy-start(bf16[4,128,128]{2,1,0:T(8,128)(2,1)S(1)} %collective-permute-done.6) | copy-start | bytes 393220
  110.7 8.0 %collective-permute-start.7 = (bf16[4,128,128]{2,1,0:T(8,128)(2,1)S(1)}, bf16[4,128,128]{2,1,0:T(8,128)(2,1)S(1)}, u32[]{:S(2)}, u32[]{:S(2)}) collective-permute-start(bf16[4,128,128]{2,1,0:T(8,128)(2,1)S(1)} %fusion.27), channel_id=1, source_target_pairs={{0,16},{4,20},{8,24},{12,28},{16,0},{20,4},{24,8},{28,12},{32,48},... | collective-permute-start | bytes 393224 | tf_op jit(solution)/shard_map/ppermute | solution.py:11
  113.9 6.9 %collective-permute-start.2 = (bf16[4,128,128]{2,1,0:T(8,128)(2,1)S(1)}, bf16[4,128,128]{2,1,0:T(8,128)(2,1)S(1)}, u32[]{:S(2)}, u32[]{:S(2)}) collective-permute-start(bf16[4,128,128]{2,1,0:T(8,128)(2,1)S(1)} %fusion.26), channel_id=1, source_target_pairs={{0,16},{4,20},{8,24},{12,28},{16,0},{20,4},{24,8},{28,12},{32,48},... | collective-permute-start | bytes 393224 | tf_op jit(solution)/shard_map/ppermute | solution.py:11
  118.6 18.6 %copy-start.4 = (bf16[4,128,128]{2,1,0:T(8,128)(2,1)}, bf16[4,128,128]{2,1,0:T(8,128)(2,1)S(1)}, u32[]{:S(2)}) copy-start(bf16[4,128,128]{2,1,0:T(8,128)(2,1)S(1)} %collective-permute-done.7) | copy-start | bytes 393220
  118.7 6.3 %collective-permute-start.8 = (bf16[4,128,128]{2,1,0:T(8,128)(2,1)S(1)}, bf16[4,128,128]{2,1,0:T(8,128)(2,1)S(1)}, u32[]{:S(2)}, u32[]{:S(2)}) collective-permute-start(bf16[4,128,128]{2,1,0:T(8,128)(2,1)S(1)} %fusion.25), channel_id=1, source_target_pairs={{0,32},{4,36},{8,40},{12,44},{16,48},{20,52},{24,56},{28,60},{32,0... | collective-permute-start | bytes 393224 | tf_op jit(solution)/shard_map/ppermute | solution.py:11
  120.8 16.5 %copy-start.3 = (bf16[4,128,128]{2,1,0:T(8,128)(2,1)}, bf16[4,128,128]{2,1,0:T(8,128)(2,1)S(1)}, u32[]{:S(2)}) copy-start(bf16[4,128,128]{2,1,0:T(8,128)(2,1)S(1)} %collective-permute-done.2) | copy-start | bytes 393220
  120.8 8.4 %collective-permute-start.3 = (bf16[4,128,128]{2,1,0:T(8,128)(2,1)S(1)}, bf16[4,128,128]{2,1,0:T(8,128)(2,1)S(1)}, u32[]{:S(2)}, u32[]{:S(2)}) collective-permute-start(bf16[4,128,128]{2,1,0:T(8,128)(2,1)S(1)} %fusion.23), channel_id=1, source_target_pairs={{0,32},{4,36},{8,40},{12,44},{16,48},{20,52},{24,56},{28,60},{32,0... | collective-permute-start | bytes 393224 | tf_op jit(solution)/shard_map/ppermute | solution.py:11
  125.0 12.2 %copy-start.6 = (bf16[4,128,128]{2,1,0:T(8,128)(2,1)}, bf16[4,128,128]{2,1,0:T(8,128)(2,1)S(1)}, u32[]{:S(2)}) copy-start(bf16[4,128,128]{2,1,0:T(8,128)(2,1)S(1)} %collective-permute-done.8) | copy-start | bytes 393220
  125.1 9.1 %collective-permute-start.9 = (bf16[4,128,128]{2,1,0:T(8,128)(2,1)S(1)}, bf16[4,128,128]{2,1,0:T(8,128)(2,1)S(1)}, u32[]{:S(2)}, u32[]{:S(2)}) collective-permute-start(bf16[4,128,128]{2,1,0:T(8,128)(2,1)S(1)} %fusion.21), channel_id=1, source_target_pairs={{0,64},{4,68},{8,72},{12,76},{16,80},{20,84},{24,88},{28,92},{32,9... | collective-permute-start | bytes 393224 | tf_op jit(solution)/shard_map/ppermute | solution.py:11
  129.3 8.0 %copy-start.5 = (bf16[4,128,128]{2,1,0:T(8,128)(2,1)}, bf16[4,128,128]{2,1,0:T(8,128)(2,1)S(1)}, u32[]{:S(2)}) copy-start(bf16[4,128,128]{2,1,0:T(8,128)(2,1)S(1)} %collective-permute-done.3) | copy-start | bytes 393220
  129.4 7.9 %collective-permute-start.4 = (bf16[4,128,128]{2,1,0:T(8,128)(2,1)S(1)}, bf16[4,128,128]{2,1,0:T(8,128)(2,1)S(1)}, u32[]{:S(2)}, u32[]{:S(2)}) collective-permute-start(bf16[4,128,128]{2,1,0:T(8,128)(2,1)S(1)} %fusion.11), channel_id=1, source_target_pairs={{0,64},{4,68},{8,72},{12,76},{16,80},{20,84},{24,88},{28,92},{32,9... | collective-permute-start | bytes 393224 | tf_op jit(solution)/shard_map/ppermute | solution.py:11
  134.2 3.0 %copy-start.10 = (bf16[4,128,128]{2,1,0:T(8,128)(2,1)}, bf16[4,128,128]{2,1,0:T(8,128)(2,1)S(1)}, u32[]{:S(2)}) copy-start(bf16[4,128,128]{2,1,0:T(8,128)(2,1)S(1)} %collective-permute-done.9) | copy-start | bytes 393220
  (2 other events, 4.3 us)
